TPU v7x, 128 devices: a whole 4x4x4 slice. The times are simulated.
128 devices in a mesh: fsdp: 16 (over x, z), dp: 8 (over y, core).
Axes of the slice: x: 4, y: 4, z: 4, core: 2. Of those that a mesh axis runs over, the one named last changes fastest.
Arguments:
- grad_parts: bfloat16 [8, 16384, 2048], P('dp', 'fsdp'), may hold values from -6 to 6
- old_master: float32 [16384, 2048], P(('fsdp', 'dp')), may hold values from -0.25 to 0.25
- old_mean: bfloat16 [16384, 2048], P(('fsdp', 'dp')), may hold values from -1 to 1
- old_mean_scale: bfloat16 [16384], P(('fsdp', 'dp')), may hold values from 0.049804688 to 0.5
- old_square: bfloat16 [16384, 2048], P(('fsdp', 'dp')), may hold values from 0.049804688 to 1
- old_square_scale: bfloat16 [16384], P(('fsdp', 'dp')), may hold values from 0.29882812 to 3
- old_map: int32 [16384], replicated, may hold values from 0 to 16383, as said below
Outputs:
- weights: bfloat16 [16384, 2048], P('fsdp')
- master: float32 [16384, 2048], P(('fsdp', 'dp'))
- mean_codes: bfloat16 [16384, 2048], P(('fsdp', 'dp'))
- mean_scales: bfloat16 [16384], P(('fsdp', 'dp'))
- square_codes: bfloat16 [16384, 2048], P(('fsdp', 'dp'))
- square_scales: bfloat16 [16384], P(('fsdp', 'dp'))
Inputs may be any that keep to these rules, and one draw needn't show every extreme that they name: old_map is a permutation of the old slots; old slot s lies on device s // 128 counted along fsdp+dp with fsdp major, and block b belongs to new owner b // 128 counted the same way. Every device holds exactly 128 old slots; one device holds at most 2 blocks of one new owner, and every draw has a pair with exactly 2.
All inputs are finite; a program needn't handle non-finite values. Where the computation divides by a largest or mean magnitude, that divisor is 1e-20 or more.
Results may differ from a plain program's by a relative error of at most 0.02.
Values may be sent and summed in bfloat16 or wider, within the bound.
No kernel may reach another device: no remote copies, remote signals or barrier semaphores. Data moves between devices by JAX's collectives and lax.ppermute only.
A program may use at most 64 MiB of HBM per device.

v0:
```python
import jax
import jax.numpy as jnp
from jax import lax
from jax.sharding import PartitionSpec as P


def pair_rank(owners, keyed):
    matching = owners[:, None] == owners[None, :]
    before = keyed[None, :] < keyed[:, None]
    return jnp.sum(jnp.where(matching & before, 1, 0), axis=1).astype(jnp.int32)


def route_bf16(chooser, values):
    flat_values = values.reshape((values.shape[0], -1))
    moved = jnp.dot(chooser.astype(jnp.bfloat16), flat_values, preferred_element_type=jnp.float32)
    return moved.astype(jnp.bfloat16).reshape((chooser.shape[0],) + values.shape[1:])


def route_f32(chooser, values):
    return jnp.dot(
        chooser.astype(jnp.float32),
        values,
        precision=lax.Precision.HIGHEST,
        preferred_element_type=jnp.float32,
    )


def block_peak(values):
    return (jnp.max(values, axis=1) + 1e-06).astype(jnp.bfloat16)


def local(grad_parts, old_master, old_mean, old_mean_scale, old_square, old_square_scale, old_map):
    count_all = lax.axis_size(("fsdp", "dp"))
    block_rows = old_master.shape[0]
    block_len = old_master.shape[1]
    peer_cap = max(2, 2 * block_rows // count_all)
    slot_total = count_all * peer_cap
    self_index = lax.axis_index(("fsdp", "dp"))
    gradient = lax.psum_scatter(
        grad_parts[0].astype(jnp.float32).astype(jnp.bfloat16),
        "dp",
        scatter_dimension=0,
        tiled=True,
    ).astype(jnp.float32)
    total_blocks = old_map.shape[0]
    my_slots = self_index * block_rows + jnp.arange(block_rows, dtype=jnp.int32)
    block_ids = jnp.arange(total_blocks, dtype=jnp.int32)
    held_blocks = jnp.sum(
        jnp.where(old_map[None, :] == my_slots[:, None], block_ids[None, :], 0), axis=1
    )
    target = held_blocks // block_rows
    local_pos = held_blocks % block_rows
    sent_rank = pair_rank(target, local_pos)
    wanted = lax.dynamic_slice_in_dim(old_map, self_index * block_rows, block_rows)
    source = wanted // block_rows
    got_rank = pair_rank(source, jnp.arange(block_rows, dtype=jnp.int32))
    slot_ids = jnp.arange(slot_total, dtype=jnp.int32)
    send_flat = target * peer_cap + sent_rank
    placing = slot_ids[:, None] == send_flat[None, :]
    moment_codes = jnp.stack([old_mean, old_square], axis=1)
    moment_scales = jnp.stack([old_mean_scale, old_square_scale], axis=1)
    code_buffer = route_bf16(placing, moment_codes).reshape((count_all, peer_cap, 2, block_len))
    scale_buffer = route_bf16(placing, moment_scales).reshape((count_all, peer_cap, 2))
    master_buffer = route_f32(placing, old_master).reshape((count_all, peer_cap, block_len))
    code_in, scale_in = (
        lax.all_to_all(code_buffer, ("fsdp", "dp"), split_axis=0, concat_axis=0, tiled=True),
        lax.all_to_all(scale_buffer, ("fsdp", "dp"), split_axis=0, concat_axis=0, tiled=True),
    )
    master_in = lax.all_to_all(
        master_buffer.astype(jnp.bfloat16), ("fsdp", "dp"), split_axis=0, concat_axis=0, tiled=True
    ).astype(master_buffer.dtype)
    recv_flat = source * peer_cap + got_rank
    picking = recv_flat[:, None] == slot_ids[None, :]
    code_rows = route_bf16(picking, code_in.reshape((slot_total, 2, block_len))).astype(jnp.float32)
    scale_rows = route_bf16(picking, scale_in.reshape((slot_total, 2))).astype(jnp.float32)
    weight_old = route_f32(picking, master_in.reshape((slot_total, block_len)))
    mean_old = code_rows[:, 0] * scale_rows[:, 0:1]
    square_old = code_rows[:, 1] * scale_rows[:, 1:2]
    mean_next = 0.9 * mean_old + 0.1 * gradient
    square_next = 0.95 * square_old + 0.05 * gradient * gradient
    master = weight_old - 0.05 * (mean_next / (jnp.sqrt(square_next) + 1e-08) + 0.1 * weight_old)
    mean_scales = block_peak(jnp.abs(mean_next))
    square_scales = block_peak(square_next)
    mean_codes = (mean_next / mean_scales.astype(jnp.float32)[:, None]).astype(jnp.bfloat16)
    square_codes = (square_next / square_scales.astype(jnp.float32)[:, None]).astype(jnp.bfloat16)
    weights = lax.all_gather(master.astype(jnp.bfloat16), "dp", axis=0, tiled=True)
    return (weights, master, mean_codes, mean_scales, square_codes, square_scales)


def solution(mesh):
    in_specs = (
        P("dp", "fsdp", None),
        P(("fsdp", "dp"), None),
        P(("fsdp", "dp"), None),
        P(("fsdp", "dp")),
        P(("fsdp", "dp"), None),
        P(("fsdp", "dp")),
        P(),
    )
    out_specs = (
        P("fsdp", None),
        P(("fsdp", "dp"), None),
        P(("fsdp", "dp"), None),
        P(("fsdp", "dp")),
        P(("fsdp", "dp"), None),
        P(("fsdp", "dp")),
    )
    return jax.shard_map(local, mesh=mesh, in_specs=in_specs, out_specs=out_specs, check_vma=False)
```

profile of v0, /device:TPU:1, one launch (start us, length us, event | category | flops | bytes accessed | tf_op | source)
XLA Modules:
  0.0 145.3 jit_solution(600305273660461602)
XLA Ops:
  8.1 1.3 select_reduce_fusion
  10.0 0.7 copy.29
  10.7 11.5 %all-to-all-start.2 = ((bf16[128,2,2]{1,2,0:T(2,128)(2,1)}), bf16[128,2,2]{1,2,0:T(2,128)(2,1)S(1)}, u32[]{:S(2)}, u32[]{:S(2)}) async-start(bf16[128,2,2]{1,2,0:T(2,128)(2,1)} %copy.29), calls=%async_computation.2 | async-start | bytes 131072 | tf_op jit(solution)/shard_map/all_to_all | solution.py:67
  22.2 1.0 convolution_convert_fusion.2
  23.3 1.5 %convert_element_type.77 = bf16[128,2,2048]{2,1,0:T(2,128)(2,1)} reshape(bf16[256,2048]{1,0:T(8,128)(2,1)S(1)} %convolution_convert_fusion.2) | data formatting | bytes 2097152 | tf_op jit(solution)/shard_map/convert_element_type | solution.py:70
  24.8 6.9 %all-to-all-done.2 = bf16[128,2,2]{1,2,0:T(2,128)(2,1)S(1)} async-done(((bf16[128,2,2]{1,2,0:T(2,128)(2,1)}), bf16[128,2,2]{1,2,0:T(2,128)(2,1)S(1)}, u32[]{:S(2)}, u32[]{:S(2)}) %all-to-all-start.2) | async-done | bytes 1056 | tf_op jit(solution)/shard_map/all_to_all | solution.py:67
  31.7 5.4 %all-to-all-start = ((bf16[128,2,2048]{2,1,0:T(2,128)(2,1)}), bf16[128,2,2048]{2,1,0:T(2,128)(2,1)}, u32[]{:S(2)}, u32[]{:S(2)}) async-start(bf16[128,2,2048]{2,1,0:T(2,128)(2,1)} %convert_element_type.77), calls=%async_computation | async-start | bytes 2097152 | tf_op jit(solution)/shard_map/all_to_all | solution.py:69
  37.7 0.7 convolution_convert_fusion
  38.4 2.8 %reshape_reshape.6 = bf16[128,2,2,2048]{3,2,1,0:T(2,128)(2,1)} reshape(bf16[256,4096]{1,0:T(8,128)(2,1)S(1)} %convolution_convert_fusion) | data formatting | bytes 4194304 | tf_op jit(solution)/shard_map/reshape;reshape | solution.py:62
  41.2 14.7 %all-to-all-done = bf16[128,2,2048]{2,1,0:T(2,128)(2,1)} async-done(((bf16[128,2,2048]{2,1,0:T(2,128)(2,1)}), bf16[128,2,2048]{2,1,0:T(2,128)(2,1)}, u32[]{:S(2)}, u32[]{:S(2)}) %all-to-all-start) | async-done | bytes 1048608 | tf_op jit(solution)/shard_map/all_to_all | solution.py:69
  55.9 5.8 %all-to-all-start.1 = ((bf16[128,2,2,2048]{3,2,1,0:T(2,128)(2,1)}), bf16[128,2,2,2048]{3,2,1,0:T(2,128)(2,1)S(1)}, u32[]{:S(2)}, u32[]{:S(2)}) async-start(bf16[128,2,2,2048]{3,2,1,0:T(2,128)(2,1)} %reshape_reshape.6), calls=%async_computation.1 | async-start | bytes 4194304 | tf_op jit(solution)/shard_map/all_to_all | solution.py:66
  62.6 2.3 %reshape.113 = bf16[256,2048]{1,0:T(8,128)(2,1)} reshape(bf16[128,2,2048]{2,1,0:T(2,128)(2,1)} %all-to-all-done) | data formatting | bytes 2097152 | tf_op jit(solution)/shard_map/reshape | solution.py:76
  64.9 27.1 %all-to-all-done.1 = bf16[128,2,2,2048]{3,2,1,0:T(2,128)(2,1)S(1)} async-done(((bf16[128,2,2,2048]{3,2,1,0:T(2,128)(2,1)}), bf16[128,2,2,2048]{3,2,1,0:T(2,128)(2,1)S(1)}, u32[]{:S(2)}, u32[]{:S(2)}) %all-to-all-start.1) | async-done | bytes 2097184 | tf_op jit(solution)/shard_map/all_to_all | solution.py:66
  92.1 0.9 copy.34
  93.0 1.8 %fusion = f32[128,4096]{1,0:T(8,128)} fusion(bf16[256,4096]{1,0:T(8,128)(2,1)S(1)} %bitcast.49, s32[128]{0:T(128)S(1)} %multiply_add_fusion.1), kind=kOutput, calls=%fused_computation.3 | convolution fusion | flops 269516800 | bytes 4194816 | tf_op jit(solution)/shard_map/dot_general | solution.py:15
  94.8 1.9 %copy.27 = f32[128,4096]{0,1:T(8,128)S(1)} copy(f32[128,4096]{1,0:T(8,128)} %fusion) | data formatting | bytes 4194304 | tf_op jit(solution)/shard_map/convert_element_type | solution.py:74
  96.7 1.5 fusion.21
  98.1 1.6 %copy.33 = f32[128,1,2048]{2,0,1:T(8,128)S(1)} copy(f32[128,1,2048]{0,2,1:T(8,128)} %get-tuple-element.12) | data formatting | bytes 2097152
  99.7 1.6 %copy.32 = f32[128,1,2048]{2,0,1:T(8,128)S(1)} copy(f32[128,1,2048]{0,2,1:T(8,128)} %get-tuple-element.13) | data formatting | bytes 2097152
  101.3 3.5 %fusion.22 = (bf16[128,2048]{1,0:T(8,128)(2,1)}, f32[128,2048]{1,0:T(8,128)}) fusion(f32[128]{0:T(128)S(1)} %get-tuple-element.16, f32[128,1,2048]{2,0,1:T(8,128)S(1)} %copy.33, bf16[128,2048]{1,0:T(8,128)(2,1)} %reduce-scatter.2.cloned.1.call-done, f32[128]{0:T(128)S(1)} %get-tuple-element.17, f32[128,1,2048]{2,0,1:T(8,128)S(1)} %copy.32, ...), kind=kOutput, calls=%fused_computation.58 | convolution fusion | flops 138706944 | bytes 5244416 | tf_op jit(solution)/shard_map/dot_general | solution.py:20
  104.9 1.7 %fusion.18 = (f32[128]{0:T(128)S(1)}, f32[128]{0:T(128)S(1)}) fusion(bf16[128,2048]{1,0:T(8,128)(2,1)} %reduce-scatter.2.cloned.1.call-done, f32[128]{0:T(128)S(1)} %get-tuple-element.16, f32[128,1,2048]{2,0,1:T(8,128)S(1)} %copy.33, f32[128]{0:T(128)S(1)} %get-tuple-element.17, f32[128,1,2048]{2,0,1:T(8,128)S(1)} %copy.32), kind=kLoop, calls=%fused_computation.54 | loop fusion | flops 3407616 | bytes 2623488 | tf_op jit(solution)/shard_map/reduce_max | solution.py:29
  107.1 1.4 divide_convert_fusion
  108.5 25.1 %all-gather.2.cloned.1.call-done = bf16[1024,2048]{1,0:T(8,128)(2,1)} async-done(((bf16[128,2048]{1,0:T(8,128)(2,1)}), bf16[1024,2048]{1,0:T(8,128)(2,1)}) %all-gather.2.cloned.1.call-update) | async-done | bytes 4194320 | tf_op jit(solution)/shard_map/all_gather | solution.py:86
  133.6 4.8 %copy.36 = bf16[1024,2048]{1,0:T(8,128)(2,1)} copy(bf16[1024,2048]{1,0:T(8,128)(2,1)} %all-gather.2.cloned.1.call-done) | data formatting | bytes 8388608
  (36 shorter events, 3.6 us)
Async XLA Ops:
  7.2 15.1 %copy-start = (f32[128,2048]{1,0:T(8,128)S(1)}, f32[128,2048]{1,0:T(8,128)}, u32[]{:S(2)}) copy-start(f32[128,2048]{1,0:T(8,128)} %param.8) | copy-start | bytes 3145732
  7.2 94.1 %reduce-scatter.2.cloned.1.call-start = ((), (), s32[]{:S(2)}) async-start(), calls=%async_computation.4 | async-start | bytes 4718592 | tf_op jit(solution)/shard_map/reduce_scatter | solution.py:39
  7.2 0.9 copy-start.4
  7.2 2.4 %copy-start.5 = (bf16[128]{0:T(256)(128)(2,1)S(1)}, bf16[128]{0:T(256)(128)(2,1)}, u32[]{:S(2)}) copy-start(bf16[128]{0:T(256)(128)(2,1)} %param.12) | copy-start | bytes 772
  7.2 2.4 %copy-start.6 = (bf16[128]{0:T(256)(128)(2,1)S(1)}, bf16[128]{0:T(256)(128)(2,1)}, u32[]{:S(2)}) copy-start(bf16[128]{0:T(256)(128)(2,1)} %param.10) | copy-start | bytes 772
  10.7 20.9 %all-to-all-start.2 = ((bf16[128,2,2]{1,2,0:T(2,128)(2,1)}), bf16[128,2,2]{1,2,0:T(2,128)(2,1)S(1)}, u32[]{:S(2)}, u32[]{:S(2)}) async-start(bf16[128,2,2]{1,2,0:T(2,128)(2,1)} %copy.29), calls=%async_computation.2 | async-start | bytes 131072 | tf_op jit(solution)/shard_map/all_to_all | solution.py:67
  23.3 13.8 %copy-start.2 = (bf16[128,2048]{1,0:T(8,128)(2,1)S(1)}, bf16[128,2048]{1,0:T(8,128)(2,1)}, u32[]{:S(2)}) copy-start(bf16[128,2048]{1,0:T(8,128)(2,1)} %param.9) | copy-start | bytes 1572868
  23.3 14.0 %copy-start.3 = (bf16[128,2048]{1,0:T(8,128)(2,1)S(1)}, bf16[128,2048]{1,0:T(8,128)(2,1)}, u32[]{:S(2)}) copy-start(bf16[128,2048]{1,0:T(8,128)(2,1)} %param.11) | copy-start | bytes 1572868
  31.7 24.2 %all-to-all-start = ((bf16[128,2,2048]{2,1,0:T(2,128)(2,1)}), bf16[128,2,2048]{2,1,0:T(2,128)(2,1)}, u32[]{:S(2)}, u32[]{:S(2)}) async-start(bf16[128,2,2048]{2,1,0:T(2,128)(2,1)} %convert_element_type.77), calls=%async_computation | async-start | bytes 2097152 | tf_op jit(solution)/shard_map/all_to_all | solution.py:69
  55.9 36.2 %all-to-all-start.1 = ((bf16[128,2,2,2048]{3,2,1,0:T(2,128)(2,1)}), bf16[128,2,2,2048]{3,2,1,0:T(2,128)(2,1)S(1)}, u32[]{:S(2)}, u32[]{:S(2)}) async-start(bf16[128,2,2,2048]{3,2,1,0:T(2,128)(2,1)} %reshape_reshape.6), calls=%async_computation.1 | async-start | bytes 4194304 | tf_op jit(solution)/shard_map/all_to_all | solution.py:66
  61.7 72.0 %all-gather.2.cloned.1.call-start = ((), (), s32[]{:S(2)}) async-start(), calls=%async_computation.5 | async-start | bytes 4718592 | tf_op jit(solution)/shard_map/all_gather | solution.py:86
  104.9 2.2 %copy-start.1 = (bf16[128,2048]{1,0:T(8,128)(2,1)S(1)}, bf16[128,2048]{1,0:T(8,128)(2,1)}, u32[]{:S(2)}) copy-start(bf16[128,2048]{1,0:T(8,128)(2,1)} %reduce-scatter.2.cloned.1.call-done) | copy-start | bytes 1572868
Sparse Core Ops, SparseCore 0:
  10.4 50.0 reduce-scatter.1
  105.0 28.6 all-gather.1
where the time goes:
time: 146 us; the launch traced here: 145 us
  waiting for transfers between devices  74.5 us (51%)
  starting transfers between devices  22.9 us (16%)
  local copies, waits for them, and re-layouts  20.5 us (14%)
  between operations  14.3 us (10%)
  matrix products  7.42 us (5%)
  other arithmetic  5.6 us (4%)
    all_to_all x1, waiting for transfers between devices, local(): lax.all_to_all(code_buffer, ('fsdp', 'dp'), split_axis=0, concat_axis=0,...  27.1 us
    all_gather x1, waiting for transfers between devices, local(): lax.all_gather(master.astype(jnp.bfloat16), 'dp', axis=0, tiled=True)  25.1 us
    all_to_all x1, waiting for transfers between devices, local(): lax.all_to_all(master_buffer.astype(jnp.bfloat16), ('fsdp', 'dp'), split_...  14.7 us
    all_to_all x1, starting transfers between devices, local(): lax.all_to_all(scale_buffer, ('fsdp', 'dp'), split_axis=0, concat_axis=0,...  11.5 us
    unnamed x20, local copies, waits for them, and re-layouts  9.58 us
    all_to_all x1, waiting for transfers between devices, local(): lax.all_to_all(scale_buffer, ('fsdp', 'dp'), split_axis=0, concat_axis=0,...  6.87 us
    all_to_all x1, starting transfers between devices, local(): lax.all_to_all(code_buffer, ('fsdp', 'dp'), split_axis=0, concat_axis=0,...  5.78 us
    all_to_all x1, starting transfers between devices, local(): lax.all_to_all(master_buffer.astype(jnp.bfloat16), ('fsdp', 'dp'), split_...  5.36 us
  transfers between devices with their start and end apart: 5, of which 4 were waited for; matrix products, arithmetic and copies ran while one was open for 17% of the time, Pallas kernels for 0%

commit v1 on v0

--- a/solution.py
+++ b/solution.py
@@ -2,6 +2,22 @@
 import jax.numpy as jnp
 from jax import lax
 from jax.sharding import PartitionSpec as P
+
+
+def gather_around(x, axis, dim):
+    ways, here, step = (lax.axis_size(axis), lax.axis_index(axis), x.shape[dim])
+    lengths = [n * ways if d == dim else n for d, n in enumerate(x.shape)]
+    full = lax.dynamic_update_slice_in_dim(jnp.zeros(lengths, x.dtype), x, here * step, axis=dim)
+    going_up = going_down = x
+    for far in range(1, ways // 2 + 1):
+        going_up = lax.ppermute(going_up, axis, [(d, (d + 1) % ways) for d in range(ways)])
+        full = lax.dynamic_update_slice_in_dim(full, going_up, (here - far) % ways * step, axis=dim)
+        if 2 * far < ways:
+            going_down = lax.ppermute(going_down, axis, [(d, (d - 1) % ways) for d in range(ways)])
+            full = lax.dynamic_update_slice_in_dim(
+                full, going_down, (here + far) % ways * step, axis=dim
+            )
+    return full
 
 
 def pair_rank(owners, keyed):
@@ -83,7 +99,7 @@
     square_scales = block_peak(square_next)
     mean_codes = (mean_next / mean_scales.astype(jnp.float32)[:, None]).astype(jnp.bfloat16)
     square_codes = (square_next / square_scales.astype(jnp.float32)[:, None]).astype(jnp.bfloat16)
-    weights = lax.all_gather(master.astype(jnp.bfloat16), "dp", axis=0, tiled=True)
+    weights = gather_around(master.astype(jnp.bfloat16), "dp", 0)
     return (weights, master, mean_codes, mean_scales, square_codes, square_scales)
 
 

time: 146 us -> 154 us (1.055)
  the two profiles are of different devices: /device:TPU:1 before, /device:TPU:0 now
where the time goes in v1:
time: 154 us; the launch traced here: 153 us
  waiting for transfers between devices  68.5 us (44%)
  starting transfers between devices  31.7 us (21%)
  local copies, waits for them, and re-layouts  26.1 us (17%)
  between operations  14.3 us (9%)
  other arithmetic  6.57 us (4%)
  matrix products  6.23 us (4%)
    all_to_all x1, waiting for transfers between devices, local(): lax.all_to_all(code_buffer, ('fsdp', 'dp'), split_axis=0, concat_axis=0,...  27.2 us
    ppermute x4, waiting for transfers between devices, gather_around(): lax.ppermute(going_up, axis, [(d, (d + 1) % ways) for d in range(ways)])  17.3 us
    all_to_all x1, waiting for transfers between devices, local(): lax.all_to_all(master_buffer.astype(jnp.bfloat16), ('fsdp', 'dp'), split_...  14.6 us
    all_to_all x1, starting transfers between devices, local(): lax.all_to_all(scale_buffer, ('fsdp', 'dp'), split_axis=0, concat_axis=0,...  11.1 us
    ppermute x3, starting transfers between devices, gather_around(): lax.ppermute(going_down, axis, [(d, (d - 1) % ways) for d in range(ways)])  8.86 us
    all_to_all x1, waiting for transfers between devices, local(): lax.all_to_all(scale_buffer, ('fsdp', 'dp'), split_axis=0, concat_axis=0,...  6.71 us
    all_to_all x1, starting transfers between devices, local(): lax.all_to_all(code_buffer, ('fsdp', 'dp'), split_axis=0, concat_axis=0,...  5.86 us
    all_to_all x1, starting transfers between devices, local(): lax.all_to_all(master_buffer.astype(jnp.bfloat16), ('fsdp', 'dp'), split_...  5.76 us
  transfers between devices with their start and end apart: 11, of which 8 were waited for; matrix products, arithmetic and copies ran while one was open for 22% of the time, Pallas kernels for 0%

profile of v1, /device:TPU:0, one launch (start us, length us, event | category | flops | bytes accessed | tf_op | source)
XLA Modules:
  0.0 153.3 jit_solution(3978886680655335728)
XLA Ops:
  10.7 11.1 %all-to-all-start.2 = ((bf16[128,2,2]{1,2,0:T(2,128)(2,1)}), bf16[128,2,2]{1,2,0:T(2,128)(2,1)S(1)}, u32[]{:S(2)}, u32[]{:S(2)}) async-start(bf16[128,2,2]{1,2,0:T(2,128)(2,1)} %copy.29), calls=%async_computation.2 | async-start | bytes 131072 | tf_op jit(solution)/shard_map/all_to_all | solution.py:83
  24.4 6.7 %all-to-all-done.2 = bf16[128,2,2]{1,2,0:T(2,128)(2,1)S(1)} async-done(((bf16[128,2,2]{1,2,0:T(2,128)(2,1)}), bf16[128,2,2]{1,2,0:T(2,128)(2,1)S(1)}, u32[]{:S(2)}, u32[]{:S(2)}) %all-to-all-start.2) | async-done | bytes 1056 | tf_op jit(solution)/shard_map/all_to_all | solution.py:83
  31.1 5.8 %all-to-all-start = ((bf16[128,2,2048]{2,1,0:T(2,128)(2,1)}), bf16[128,2,2048]{2,1,0:T(2,128)(2,1)}, u32[]{:S(2)}, u32[]{:S(2)}) async-start(bf16[128,2,2048]{2,1,0:T(2,128)(2,1)} %convert_element_type.77), calls=%async_computation | async-start | bytes 2097152 | tf_op jit(solution)/shard_map/all_to_all | solution.py:85
  38.2 2.8 %reshape_reshape.6 = bf16[128,2,2,2048]{3,2,1,0:T(2,128)(2,1)} reshape(bf16[256,4096]{1,0:T(8,128)(2,1)S(1)} %convolution_convert_fusion) | data formatting | bytes 4194304 | tf_op jit(solution)/shard_map/reshape;reshape | solution.py:78
  41.0 14.6 %all-to-all-done = bf16[128,2,2048]{2,1,0:T(2,128)(2,1)} async-done(((bf16[128,2,2048]{2,1,0:T(2,128)(2,1)}), bf16[128,2,2048]{2,1,0:T(2,128)(2,1)}, u32[]{:S(2)}, u32[]{:S(2)}) %all-to-all-start) | async-done | bytes 1048608 | tf_op jit(solution)/shard_map/all_to_all | solution.py:85
  55.6 5.9 %all-to-all-start.1 = ((bf16[128,2,2,2048]{3,2,1,0:T(2,128)(2,1)}), bf16[128,2,2,2048]{3,2,1,0:T(2,128)(2,1)S(1)}, u32[]{:S(2)}, u32[]{:S(2)}) async-start(bf16[128,2,2,2048]{3,2,1,0:T(2,128)(2,1)} %reshape_reshape.6), calls=%async_computation.1 | async-start | bytes 4194304 | tf_op jit(solution)/shard_map/all_to_all | solution.py:82
  62.2 2.3 %reshape.113 = bf16[256,2048]{1,0:T(8,128)(2,1)} reshape(bf16[128,2,2048]{2,1,0:T(2,128)(2,1)} %all-to-all-done) | data formatting | bytes 2097152 | tf_op jit(solution)/shard_map/reshape | solution.py:92
  64.5 27.2 %all-to-all-done.1 = bf16[128,2,2,2048]{3,2,1,0:T(2,128)(2,1)S(1)} async-done(((bf16[128,2,2,2048]{3,2,1,0:T(2,128)(2,1)}), bf16[128,2,2,2048]{3,2,1,0:T(2,128)(2,1)S(1)}, u32[]{:S(2)}, u32[]{:S(2)}) %all-to-all-start.1) | async-done | bytes 2097184 | tf_op jit(solution)/shard_map/all_to_all | solution.py:82
  92.6 1.8 %fusion = f32[128,4096]{1,0:T(8,128)} fusion(bf16[256,4096]{1,0:T(8,128)(2,1)S(1)} %bitcast.49, s32[128]{0:T(128)S(1)} %multiply_add_fusion.1), kind=kOutput, calls=%fused_computation.3 | convolution fusion | flops 269516800 | bytes 4194816 | tf_op jit(solution)/shard_map/dot_general | solution.py:31
  94.4 1.9 %copy.27 = f32[128,4096]{0,1:T(8,128)S(1)} copy(f32[128,4096]{1,0:T(8,128)} %fusion) | data formatting | bytes 4194304 | tf_op jit(solution)/shard_map/convert_element_type | solution.py:90
  101.0 2.5 %broadcast_in_dim.24 = bf16[1024,2048]{1,0:T(8,128)(2,1)} broadcast(bf16[]{:T(256)} %constant.91.clone.1), dimensions={} | broadcast | bytes 4194306 | tf_op jit(solution)/shard_map/broadcast_in_dim | solution.py:10
  103.5 2.3 %constant_dynamic-update-slice_fusion.6 = (bf16[1024,2048]{1,0:T(8,128)(2,1)}, bf16[128,2048]{1,0:T(8,128)(2,1)}, f32[128,2048]{1,0:T(8,128)}) fusion(bf16[1024,2048]{1,0:T(8,128)(2,1)} %broadcast_in_dim.24, s32[]{:T(128)S(6)} %select_n.109, f32[128]{0:T(128)S(1)} %get-tuple-element.18, f32[128,1,2048]{2,0,1:T(8,128)S(1)} %copy.33, ...), kind=kOutput, calls=%fused_computation.40 | convolution fusion | flops 138706944 | bytes 5768708 | tf_op jit(solution)/shard_map/dot_general | solution.py:36
  105.9 3.0 %collective-permute-start.1 = (bf16[128,2048]{1,0:T(8,128)(2,1)}, bf16[128,2048]{1,0:T(8,128)(2,1)}, u32[]{:S(2)}, u32[]{:S(2)}) collective-permute-start(bf16[128,2048]{1,0:T(8,128)(2,1)} %get-tuple-element.13), channel_id=1, source_target_pairs={{0,7},{1,0},{2,1},{3,2},{4,3},{5,4},{6,5},{7,6},{8,15},{9,8},{10,9... | collective-permute-start | bytes 1572872 | tf_op jit(solution)/shard_map/ppermute | solution.py:16
  108.8 1.6 %fusion.18 = (f32[128]{0:T(128)S(1)}, f32[128]{0:T(128)S(1)}) fusion(bf16[128,2048]{1,0:T(8,128)(2,1)} %reduce-scatter.2.cloned.1.call-done, f32[128]{0:T(128)S(1)} %get-tuple-element.18, f32[128,1,2048]{2,0,1:T(8,128)S(1)} %copy.33, f32[128]{0:T(128)S(1)} %get-tuple-element.19, f32[128,1,2048]{2,0,1:T(8,128)S(1)} %copy.32), kind=kLoop, calls=%fused_computation.62 | loop fusion | flops 3407616 | bytes 2623488 | tf_op jit(solution)/shard_map/reduce_max | solution.py:45
  110.9 5.0 %collective-permute-done = bf16[128,2048]{1,0:T(8,128)(2,1)} collective-permute-done((bf16[128,2048]{1,0:T(8,128)(2,1)}, bf16[128,2048]{1,0:T(8,128)(2,1)}, u32[]{:S(2)}, u32[]{:S(2)}) %collective-permute-start) | collective-permute-done | bytes 524320 | tf_op jit(solution)/shard_map/ppermute | solution.py:13
  116.0 3.0 %collective-permute-start.3 = (bf16[128,2048]{1,0:T(8,128)(2,1)}, bf16[128,2048]{1,0:T(8,128)(2,1)S(1)}, u32[]{:S(2)}, u32[]{:S(2)}) collective-permute-start(bf16[128,2048]{1,0:T(8,128)(2,1)} %collective-permute-done.1), channel_id=1, source_target_pairs={{0,7},{1,0},{2,1},{3,2},{4,3},{5,4},{6,5},{7,6},{8,15},{9,8},{10,9... | collective-permute-start | bytes 1572872 | tf_op jit(solution)/shard_map/ppermute | solution.py:16
  119.0 2.5 %divide_convert_fusion = (bf16[128,2048]{1,0:T(8,128)(2,1)}, bf16[128,2048]{1,0:T(8,128)(2,1)}) fusion(f32[128]{0:T(128)S(1)} %get-tuple-element.8, bf16[128,2048]{1,0:T(8,128)(2,1)} %reduce-scatter.2.cloned.1.call-done, f32[128]{0:T(128)S(1)} %get-tuple-element.18, f32[128,1,2048]{2,0,1:T(8,128)S(1)} %copy.33, f32[128]{0:T(128)S(1)} %get-tuple-element.23, ...), kind=kLoop, calls=%fused_computation.17 | loop fusion | flops 3670016 | bytes 3672064 | tf_op jit(solution)/shard_map/convert_element_type | solution.py:101
  121.4 4.6 %collective-permute-done.2 = bf16[128,2048]{1,0:T(8,128)(2,1)S(1)} collective-permute-done((bf16[128,2048]{1,0:T(8,128)(2,1)}, bf16[128,2048]{1,0:T(8,128)(2,1)S(1)}, u32[]{:S(2)}, u32[]{:S(2)}) %collective-permute-start.2) | collective-permute-done | bytes 524320 | tf_op jit(solution)/shard_map/ppermute | solution.py:13
  126.0 1.9 %constant_dynamic-update-slice_fusion.5 = bf16[1024,2048]{1,0:T(8,128)(2,1)} fusion(bf16[1024,2048]{1,0:T(8,128)(2,1)} %get-tuple-element.12, bf16[128,2048]{1,0:T(8,128)(2,1)} %collective-permute-done, s32[]{:T(128)S(6)} %select_n.111), kind=kLoop, calls=%fused_computation.39 | loop fusion | bytes 1048580 | tf_op jit(solution)/shard_map/dynamic_update_slice | solution.py:14
  127.9 1.9 %constant_dynamic-update-slice_fusion.4 = bf16[1024,2048]{1,0:T(8,128)(2,1)} fusion(bf16[1024,2048]{1,0:T(8,128)(2,1)} %constant_dynamic-update-slice_fusion.5, bf16[128,2048]{1,0:T(8,128)(2,1)} %collective-permute-done.1, s32[]{:T(128)S(6)} %select_n.113), kind=kLoop, calls=%fused_computation.38 | loop fusion | bytes 1048580 | tf_op jit(solution)/shard_map/dynamic_update_slice | solution.py:17
  129.8 3.0 %collective-permute-start.5 = (bf16[128,2048]{1,0:T(8,128)(2,1)S(1)}, bf16[128,2048]{1,0:T(8,128)(2,1)S(1)}, u32[]{:S(2)}, u32[]{:S(2)}) collective-permute-start(bf16[128,2048]{1,0:T(8,128)(2,1)S(1)} %collective-permute-done.3), channel_id=1, source_target_pairs={{0,7},{1,0},{2,1},{3,2},{4,3},{5,4},{6,5},{7,6},{8,15},{9,8},{10,9... | collective-permute-start | bytes 1572872 | tf_op jit(solution)/shard_map/ppermute | solution.py:16
  133.6 2.3 %collective-permute-done.4 = bf16[128,2048]{1,0:T(8,128)(2,1)S(1)} collective-permute-done((bf16[128,2048]{1,0:T(8,128)(2,1)S(1)}, bf16[128,2048]{1,0:T(8,128)(2,1)S(1)}, u32[]{:S(2)}, u32[]{:S(2)}) %collective-permute-start.4) | collective-permute-done | bytes 524320 | tf_op jit(solution)/shard_map/ppermute | solution.py:13
  137.5 1.9 %collective-permute-done.5 = bf16[128,2048]{1,0:T(8,128)(2,1)S(1)} collective-permute-done((bf16[128,2048]{1,0:T(8,128)(2,1)S(1)}, bf16[128,2048]{1,0:T(8,128)(2,1)S(1)}, u32[]{:S(2)}, u32[]{:S(2)}) %collective-permute-start.5) | collective-permute-done | bytes 524320 | tf_op jit(solution)/shard_map/ppermute | solution.py:16
  140.3 5.4 %collective-permute-done.6 = bf16[128,2048]{1,0:T(8,128)(2,1)S(1)} collective-permute-done((bf16[128,2048]{1,0:T(8,128)(2,1)S(1)}, bf16[128,2048]{1,0:T(8,128)(2,1)S(1)}, u32[]{:S(2)}, u32[]{:S(2)}) %collective-permute-start.6) | collective-permute-done | bytes 524320 | tf_op jit(solution)/shard_map/ppermute | solution.py:13
  (56 shorter events, 18.2 us)
Async XLA Ops:
  7.2 14.7 %copy-start = (f32[128,2048]{1,0:T(8,128)S(1)}, f32[128,2048]{1,0:T(8,128)}, u32[]{:S(2)}) copy-start(f32[128,2048]{1,0:T(8,128)} %param.8) | copy-start | bytes 3145732
  7.2 0.9 copy-start.5
  7.2 2.4 %copy-start.6 = (bf16[128]{0:T(256)(128)(2,1)S(1)}, bf16[128]{0:T(256)(128)(2,1)}, u32[]{:S(2)}) copy-start(bf16[128]{0:T(256)(128)(2,1)} %param.12) | copy-start | bytes 772
  7.2 2.4 %copy-start.7 = (bf16[128]{0:T(256)(128)(2,1)S(1)}, bf16[128]{0:T(256)(128)(2,1)}, u32[]{:S(2)}) copy-start(bf16[128]{0:T(256)(128)(2,1)} %param.10) | copy-start | bytes 772
  7.2 93.7 %reduce-scatter.2.cloned.1.call-start = ((), (), s32[]{:S(2)}) async-start(), calls=%async_computation.4 | async-start | bytes 4718592 | tf_op jit(solution)/shard_map/reduce_scatter | solution.py:55
  7.9 28.9 %copy-start.3 = (bf16[128,2048]{1,0:T(8,128)(2,1)S(1)}, bf16[128,2048]{1,0:T(8,128)(2,1)}, u32[]{:S(2)}) copy-start(bf16[128,2048]{1,0:T(8,128)(2,1)} %param.11) | copy-start | bytes 1572868
  8.0 29.2 %copy-start.4 = (bf16[128,2048]{1,0:T(8,128)(2,1)S(1)}, bf16[128,2048]{1,0:T(8,128)(2,1)}, u32[]{:S(2)}) copy-start(bf16[128,2048]{1,0:T(8,128)(2,1)} %param.9) | copy-start | bytes 1572868
  10.7 20.4 %all-to-all-start.2 = ((bf16[128,2,2]{1,2,0:T(2,128)(2,1)}), bf16[128,2,2]{1,2,0:T(2,128)(2,1)S(1)}, u32[]{:S(2)}, u32[]{:S(2)}) async-start(bf16[128,2,2]{1,2,0:T(2,128)(2,1)} %copy.29), calls=%async_computation.2 | async-start | bytes 131072 | tf_op jit(solution)/shard_map/all_to_all | solution.py:83
  31.1 24.5 %all-to-all-start = ((bf16[128,2,2048]{2,1,0:T(2,128)(2,1)}), bf16[128,2,2048]{2,1,0:T(2,128)(2,1)}, u32[]{:S(2)}, u32[]{:S(2)}) async-start(bf16[128,2,2048]{2,1,0:T(2,128)(2,1)} %convert_element_type.77), calls=%async_computation | async-start | bytes 2097152 | tf_op jit(solution)/shard_map/all_to_all | solution.py:85
  55.6 36.1 %all-to-all-start.1 = ((bf16[128,2,2,2048]{3,2,1,0:T(2,128)(2,1)}), bf16[128,2,2,2048]{3,2,1,0:T(2,128)(2,1)S(1)}, u32[]{:S(2)}, u32[]{:S(2)}) async-start(bf16[128,2,2,2048]{3,2,1,0:T(2,128)(2,1)} %reshape_reshape.6), calls=%async_computation.1 | async-start | bytes 4194304 | tf_op jit(solution)/shard_map/all_to_all | solution.py:82
  101.0 2.6 %copy-start.1 = (bf16[128,2048]{1,0:T(8,128)(2,1)S(1)}, bf16[128,2048]{1,0:T(8,128)(2,1)}, u32[]{:S(2)}) copy-start(bf16[128,2048]{1,0:T(8,128)(2,1)} %reduce-scatter.2.cloned.1.call-done) | copy-start | bytes 1572868
  101.0 2.6 %copy-start.2 = (bf16[256,2048]{1,0:T(8,128)(2,1)S(1)}, bf16[256,2048]{1,0:T(8,128)(2,1)}, u32[]{:S(2)}) copy-start(bf16[256,2048]{1,0:T(8,128)(2,1)} %reshape.113) | copy-start | bytes 3145732
  105.9 10.1 %collective-permute-start = (bf16[128,2048]{1,0:T(8,128)(2,1)}, bf16[128,2048]{1,0:T(8,128)(2,1)}, u32[]{:S(2)}, u32[]{:S(2)}) collective-permute-start(bf16[128,2048]{1,0:T(8,128)(2,1)} %get-tuple-element.13), channel_id=1, source_target_pairs={{0,1},{1,2},{2,3},{3,4},{4,5},{5,6},{6,7},{7,0},{8,9},{9,10},{10,1... | collective-permute-start | bytes 1572872 | tf_op jit(solution)/shard_map/ppermute | solution.py:13
  105.9 10.1 %collective-permute-start.1 = (bf16[128,2048]{1,0:T(8,128)(2,1)}, bf16[128,2048]{1,0:T(8,128)(2,1)}, u32[]{:S(2)}, u32[]{:S(2)}) collective-permute-start(bf16[128,2048]{1,0:T(8,128)(2,1)} %get-tuple-element.13), channel_id=1, source_target_pairs={{0,7},{1,0},{2,1},{3,2},{4,3},{5,4},{6,5},{7,6},{8,15},{9,8},{10,9... | collective-permute-start | bytes 1572872 | tf_op jit(solution)/shard_map/ppermute | solution.py:16
  116.0 10.0 %collective-permute-start.2 = (bf16[128,2048]{1,0:T(8,128)(2,1)}, bf16[128,2048]{1,0:T(8,128)(2,1)S(1)}, u32[]{:S(2)}, u32[]{:S(2)}) collective-permute-start(bf16[128,2048]{1,0:T(8,128)(2,1)} %collective-permute-done), channel_id=1, source_target_pairs={{0,1},{1,2},{2,3},{3,4},{4,5},{5,6},{6,7},{7,0},{8,9},{9,10},{10,1... | collective-permute-start | bytes 1572872 | tf_op jit(solution)/shard_map/ppermute | solution.py:13
  116.0 13.8 %collective-permute-start.3 = (bf16[128,2048]{1,0:T(8,128)(2,1)}, bf16[128,2048]{1,0:T(8,128)(2,1)S(1)}, u32[]{:S(2)}, u32[]{:S(2)}) collective-permute-start(bf16[128,2048]{1,0:T(8,128)(2,1)} %collective-permute-done.1), channel_id=1, source_target_pairs={{0,7},{1,0},{2,1},{3,2},{4,3},{5,4},{6,5},{7,6},{8,15},{9,8},{10,9... | collective-permute-start | bytes 1572872 | tf_op jit(solution)/shard_map/ppermute | solution.py:16
  126.0 9.8 %collective-permute-start.4 = (bf16[128,2048]{1,0:T(8,128)(2,1)S(1)}, bf16[128,2048]{1,0:T(8,128)(2,1)S(1)}, u32[]{:S(2)}, u32[]{:S(2)}) collective-permute-start(bf16[128,2048]{1,0:T(8,128)(2,1)S(1)} %collective-permute-done.2), channel_id=1, source_target_pairs={{0,1},{1,2},{2,3},{3,4},{4,5},{5,6},{6,7},{7,0},{8,9},{9,10},{10,1... | collective-permute-start | bytes 1572872 | tf_op jit(solution)/shard_map/ppermute | solution.py:13
  129.8 9.7 %collective-permute-start.5 = (bf16[128,2048]{1,0:T(8,128)(2,1)S(1)}, bf16[128,2048]{1,0:T(8,128)(2,1)S(1)}, u32[]{:S(2)}, u32[]{:S(2)}) collective-permute-start(bf16[128,2048]{1,0:T(8,128)(2,1)S(1)} %collective-permute-done.3), channel_id=1, source_target_pairs={{0,7},{1,0},{2,1},{3,2},{4,3},{5,4},{6,5},{7,6},{8,15},{9,8},{10,9... | collective-permute-start | bytes 1572872 | tf_op jit(solution)/shard_map/ppermute | solution.py:16
  135.8 9.8 %collective-permute-start.6 = (bf16[128,2048]{1,0:T(8,128)(2,1)S(1)}, bf16[128,2048]{1,0:T(8,128)(2,1)S(1)}, u32[]{:S(2)}, u32[]{:S(2)}) collective-permute-start(bf16[128,2048]{1,0:T(8,128)(2,1)S(1)} %collective-permute-done.4), channel_id=1, source_target_pairs={{0,1},{1,2},{2,3},{3,4},{4,5},{5,6},{6,7},{7,0},{8,9},{9,10},{10,1... | collective-permute-start | bytes 1572872 | tf_op jit(solution)/shard_map/ppermute | solution.py:13
Sparse Core Ops, SparseCore 0:
  10.4 50.9 reduce-scatter.1
